TPU v7x, 32 devices: a whole 2x2x4 slice. The times are simulated.
32 devices in a mesh: dom: 8 (over z, y), sub: 4 (over x, core).
Axes of the slice: x: 2, y: 2, z: 4, core: 2. Of those that a mesh axis runs over, the one named last changes fastest.
Arguments:
- displacement: float32 [3, 128, 64, 128], P(None, 'dom', 'sub'), may hold values from -0.3 to 0.3
- velocity: float32 [3, 128, 64, 128], P(None, 'dom', 'sub'), may hold values from -6 to 6
- modulus: float32 [128, 64, 128], P('dom', 'sub'), may hold values from 0.5 to 4
- element_stiffness: bfloat16 [24, 24], replicated, may hold values from -9 to 9.5, as said below
- viscosity: float32 [], replicated, may hold values from 0.1 to 0.4
- step_size: float32 [], replicated, may hold values from 0.3 to 0.6
- seg_tilt: float32 [2, 65536], P(None, ('dom', 'sub')), may hold values from -1.5 to 1.5
- seg_offset: float32 [65536], P(('dom', 'sub')), may hold values from -0.08 to 0.04
- seg_stiffness: float32 [65536], P(('dom', 'sub')), may hold values from 4 to 40
- projection: int32 [64, 128], P(('dom', 'sub')), may hold values from 0 to 65535, as said below
- contact_flag: int32 [64, 128], P(('dom', 'sub')), may hold values from 0 to 1
- candidates: int32 [64, 8], P(('dom', 'sub')), may hold values from -1 to 63, as said below
Outputs:
- new_velocity: float32 [3, 128, 64, 128], P(None, 'dom', 'sub')
- reaction: float32 [3, 65536], P(None, ('dom', 'sub'))
Inputs may be any that keep to these rules, and one draw needn't show every extreme that they name: `element_stiffness`: symmetric with a dominant positive diagonal. `candidates`: each row lists distinct segment blocks of its own group, numbered 0 to 63 within the group, in its first 1 to 8 entries, then -1 in the rest; the rows of the node blocks of one group hold exactly 16 listed entries together (a block may appear in more than one row), and some row lists 8. `projection`: A segment of the node's own group: p // 128 lies in group * 64 to group * 64 + 63.
All inputs are finite; a program needn't handle non-finite values.
Results may differ from a plain program's by a relative error of at most 0.0026.
Values sent between devices are 32-bit elements; how exact they have to be, the bound alone decides.
A program may use at most 64 MiB of HBM per device.

v0:
```python
import functools

import jax
import jax.numpy as jnp
from jax import lax
from jax.experimental import pallas as pl
from jax.experimental.pallas import tpu as pltpu
from jax.sharding import PartitionSpec as P

MESH = pl.DeviceIdType.MESH
BLK = 128
UNROLL = 3
EARLY = 8
F32 = jnp.float32
BF16 = jnp.bfloat16
DIRS = tuple((dx, dy) for dx in (-1, 0, 1) for dy in (-1, 0, 1) if (dx, dy) != (0, 0))


def iota(shape, axis):
    return lax.broadcasted_iota(jnp.int32, shape, axis)


def split3(x):
    hi = x.astype(BF16)
    rest = x - hi.astype(F32)
    mid = rest.astype(BF16)
    low = (rest - mid.astype(F32)).astype(BF16)
    return hi, mid, low


def stiffness_maps(stiff):
    row = iota((96, 24), 0) // 8
    col = iota((96, 24), 1)
    wide = (iota((24, 192), 0) == iota((24, 192), 1) // 8).astype(BF16)
    parts = []
    for corner_y in (0, 1):
        pick = (col == (row // 2) * 4 + row % 2 + 2 * corner_y).astype(BF16)
        rows = jnp.dot(pick, stiff, preferred_element_type=F32).astype(BF16)
        parts.append(jnp.dot(rows, wide, preferred_element_type=F32))
    to_y = iota((96, 192), 0) % 8
    from_y = iota((96, 192), 1) % 8
    same = jnp.where(from_y == to_y, parts[0], 0.0) + jnp.where(from_y + 1 == to_y, parts[1], 0.0)
    carry = jnp.where((from_y == 7) & (to_y == 0), parts[1], 0.0)
    return same.astype(BF16), carry.astype(BF16)


def edge_maps(stiff, corner_y):
    row = iota((48, 24), 0) // 8
    col = iota((48, 24), 1)
    wide = (iota((24, 192), 0) == iota((24, 192), 1) // 8).astype(BF16)
    parts = []
    for corner_x in (0, 1):
        pick = (col == (row // 2) * 8 + row % 2 + 4 * corner_x + 2 * corner_y).astype(BF16)
        rows = jnp.dot(pick, stiff, preferred_element_type=F32).astype(BF16)
        parts.append(jnp.dot(rows, wide, preferred_element_type=F32))
    to_x = iota((48, 192), 0) % 8
    from_x = iota((48, 192), 1) % 8
    same = jnp.where(from_x == to_x, parts[1], 0.0) + jnp.where(from_x == to_x + 1, parts[0], 0.0)
    following = jnp.where((from_x == 0) & (to_x == 7), parts[0], 0.0)
    return same.astype(BF16), following.astype(BF16)


def kernel(
    dom_count, sub_count, visc_hbm, step_hbm, cand_hbm, stiff_hbm, tilt_hbm, off_hbm, stf_hbm, proj_hbm, flag_hbm,
    disp, vel, mod, nv_ref, react_ref, visc_ref, step_ref, cand_ref, stiff_ref, tilt_ref, proj_ref, flag_ref,
    w, md, xr, mx, msg, nodes, back_out, back, table, values, same_ref, carry_ref, edge_ref, prev,
    local_sem, halo_send, halo_recv, p1_send, p1_recv, p2_send, p2_recv,
):
    d = lax.axis_index("dom")
    s = lax.axis_index("sub")
    planes, rows, nz = disp.shape[1], disp.shape[2], disp.shape[3]
    inner = slice(1, 1 + planes)
    seg_blocks = off_hbm.shape[0]
    node_blocks = proj_ref.shape[0]
    pairs = (
        (disp, w.at[0:3, inner, 0:rows, :]),
        (vel, w.at[3:6, inner, 0:rows, :]),
        (mod, md.at[inner, :, :]),
        (proj_hbm, proj_ref),
        (flag_hbm, flag_ref),
        (cand_hbm, cand_ref),
        (stiff_hbm, stiff_ref),
        (tilt_hbm, tilt_ref),
        (off_hbm, table.at[2 * seg_blocks : 3 * seg_blocks, :]),
        (stf_hbm, table.at[3 * seg_blocks : 4 * seg_blocks, :]),
        (visc_hbm, visc_ref),
        (step_hbm, step_ref),
        (disp.at[:, :, 0, :], xr.at[1, 0:3, inner, :]),
        (vel.at[:, :, 0, :], xr.at[1, 3:6, inner, :]),
        (disp.at[:, :, rows - 1, :], xr.at[2, 0:3, inner, :]),
        (vel.at[:, :, rows - 1, :], xr.at[2, 3:6, inner, :]),
        (mod.at[:, rows - 1, :], mx.at[1, inner, :]),
    )
    local_copies = [pltpu.make_async_copy(a, b, local_sem.at[i]) for i, (a, b) in enumerate(pairs)]
    for copy in local_copies:
        copy.start()

    w[:, :, rows : rows + 8, :] = jnp.zeros((6, planes + 2, 8, nz), F32)
    for edge in (0, planes + 1):
        w[:, edge, 0:rows, :] = jnp.zeros((6, rows, nz), F32)
    md[0] = jnp.zeros((rows, nz), F32)
    for k in (0, 3):
        xr[k] = jnp.zeros(xr.shape[1:], F32)
    for k in (1, 2):
        xr[k, :, planes + 1 :, :] = jnp.zeros((6, xr.shape[2] - planes - 1, nz), F32)
    mx[0] = jnp.zeros(mx.shape[1:], F32)
    mx[1, planes + 1 :, :] = jnp.zeros((mx.shape[1] - planes - 1, nz), F32)

    def exists(dx, dy):
        cond = (d + dx >= 0) & (d + dx < dom_count)
        return cond & (s + dy >= 0) & (s + dy < sub_count)

    barrier = pltpu.get_barrier_semaphore()
    for off in range(1, sub_count):
        pl.semaphore_signal(barrier, inc=1, device_id=(d, (s + off) % sub_count), device_id_type=MESH)
    for dx, dy in DIRS:
        if dx != 0:

            @pl.when(exists(dx, dy))
            def _():
                pl.semaphore_signal(barrier, inc=1, device_id=(d + dx, s + dy), device_id_type=MESH)

    for copy in local_copies:
        copy.wait()

    block_planes = BLK // rows
    group_start = d * (seg_blocks * BLK * sub_count)
    target = proj_ref[...] - group_start
    target_block = target // BLK
    listed = jnp.zeros(target.shape, jnp.bool_)
    for slot in range(cand_ref.shape[1]):
        listed = listed | (target_block == cand_ref[:, slot : slot + 1])
    chosen = jnp.where(listed & (flag_ref[...] == 1), target, -1).astype(F32)
    for c in range(3):
        for k in range(node_blocks):
            part = w[c, 1 + k * block_planes : 1 + (k + 1) * block_planes, 0:rows, :].reshape(BLK, nz)
            msg[c, k : k + 1, :] = jnp.transpose(part)[nz - 1 : nz, :]
    msg[3] = chosen

    same, carry = stiffness_maps(stiff_ref[...])
    same_ref[...] = same
    carry_ref[...] = carry

    for b in range(seg_blocks):
        lanes = slice(b * BLK, (b + 1) * BLK)
        for c in range(2):
            table[c * seg_blocks + b : c * seg_blocks + b + 1, :] = tilt_ref[c : c + 1, lanes]
    table3 = jnp.concatenate(split3(table[...]), axis=0)

    columns = 1 + (s > 0).astype(jnp.int32) + (s < sub_count - 1).astype(jnp.int32)
    sides = (d > 0).astype(jnp.int32) + (d < dom_count - 1).astype(jnp.int32)
    pl.semaphore_wait(barrier, sub_count - 1 + columns * sides)

    def halo_copies(i):
        dx, dy = DIRS[i]
        src_x = {1: planes, -1: 1, 0: inner}[dx]
        dst_x = {1: 0, -1: planes + 1, 0: inner}[dx]
        if dy == 0:
            pairs = [(w.at[:, src_x, 0:rows, :], w.at[:, dst_x, 0:rows, :])]
            if dx > 0:
                pairs.append((md.at[src_x], md.at[dst_x]))
        else:
            src_y = rows - 1 if dy > 0 else 0
            pairs = [(w.at[:, src_x, src_y, :], xr.at[0 if dy > 0 else 3, :, dst_x, :])]
            if dx >= 0 and dy > 0:
                pairs.append((md.at[src_x, src_y, :], mx.at[0, dst_x, :]))
        return [
            pltpu.make_async_remote_copy(
                src_ref=a,
                dst_ref=b,
                send_sem=halo_send.at[i, j],
                recv_sem=halo_recv.at[i, j],
                device_id=(d + dx, s + dy),
                device_id_type=MESH,
            )
            for j, (a, b) in enumerate(pairs)
        ]

    for i, (dx, dy) in enumerate(DIRS):

        @pl.when(exists(dx, dy))
        def _():
            for copy in halo_copies(i):
                copy.start()

    def node_copy(off):
        return pltpu.make_async_remote_copy(
            src_ref=msg,
            dst_ref=nodes.at[:, node_blocks * off : node_blocks * (off + 1), :],
            send_sem=p1_send.at[off - 1],
            recv_sem=p1_recv.at[off - 1],
            device_id=(d, (s + off) % sub_count),
            device_id_type=MESH,
        )

    for off in range(1, sub_count):
        node_copy(off).start()
    nodes[:, 0:node_blocks, :] = msg[...]

    for k in (0, 1):
        same, following = edge_maps(stiff_ref[...], 1 - k)
        edge_ref[2 * k] = same
        edge_ref[2 * k + 1] = following

    viscosity = visc_ref[0]
    step = step_ref[0]
    row_blocks = rows // 8

    def element_blocks(view, modulus, mask):
        def corner_views(field, a):
            flat = [view(field, a, b) for b in (0, 1)]
            return [[x, pltpu.roll(x, nz - 1, 1)] for x in flat]

        speed = [[corner_views(3 + m, a) for a in (0, 1)] for m in range(3)]
        rate = None
        for m in range(3):
            for a in (0, 1):
                for b in (0, 1):
                    for c in (0, 1):
                        term = speed[m][a][b][c]
                        sign = (a, b, c)[m]
                        if rate is None:
                            rate = -term
                        else:
                            rate = rate + term if sign else rate - term
        bulk = (viscosity * mask) * jnp.maximum(-0.25 * rate, 0.0)
        factor = mask * modulus
        entries = []
        for m in range(3):
            for a in (0, 1):
                disps = corner_views(m, a)
                for b in (0, 1):
                    for c in (0, 1):
                        entries.append(factor * disps[b][c] + bulk * speed[m][a][b][c])
        return [
            jnp.concatenate([x[8 * t : 8 * t + 8, :] for x in entries], axis=0).astype(BF16)
            for t in range(entries[0].shape[0] // 8)
        ]

    def mapped(map_ref, blocks):
        wide = jnp.dot(map_ref[...], jnp.concatenate(blocks, axis=1), preferred_element_type=F32)
        return [wide[:, t * nz : (t + 1) * nz] for t in range(len(blocks))]

    inside_yz = ((iota((rows, nz), 0) <= rows - 2) & (iota((rows, nz), 1) <= nz - 2)).astype(F32)

    def element_plane(e, mask):
        blocks = element_blocks(lambda f, a, b: w[f, e + a, b : b + rows, :], md[e], mask)
        force = mapped(same_ref, blocks)
        carried = mapped(carry_ref, blocks[:-1]) if row_blocks > 1 else []
        return [force[0]] + [x + y for x, y in zip(force[1:], carried)]

    def part_of(force, m, a, c):
        at = ((m * 2 + a) * 2 + c) * 8
        return force[at : at + 8, :]

    def node_plane(e, force):
        for m in range(3):
            for t in range(row_blocks):
                part = [part_of(force[t], m, 0, c) + prev[m * 2 + c, t] for c in (0, 1)]
                internal = part[0] + pltpu.roll(part[1], 1, 1)
                at = slice(8 * t, 8 * t + 8)
                nv_ref[m, e - 1, at, :] = w[3 + m, e, at, :] - step * internal

    def advance(e):
        force = element_plane(e, inside_yz)
        node_plane(e, force)
        for m in range(3):
            for c in (0, 1):
                for t in range(row_blocks):
                    prev[m * 2 + c, t] = part_of(force[t], m, 1, c)

    prev[...] = jnp.zeros(prev.shape, F32)
    group = UNROLL if (planes - 1) % UNROLL == 0 else 1
    early = (planes - 1) // group * EARLY // 16

    def advance_group(g):
        for i in range(group):
            advance(1 + g * group + i)

    @pl.loop(0, early)
    def _(g):
        advance_group(g)

    for off in range(1, sub_count):
        node_copy(off).wait_recv()

    group_rows = node_blocks * sub_count
    wanted = nodes[3].astype(jnp.int32) - s * (seg_blocks * BLK)
    valid = (nodes[3] >= 0.0) & (wanted >= 0) & (wanted < seg_blocks * BLK)
    wanted = jnp.where(valid, wanted, 0)
    lane = wanted % BLK
    block = jnp.where(valid, wanted // BLK, -1)
    lane_rows = iota((BLK, BLK), 0)
    block_rows = iota((seg_blocks, BLK), 0)
    hot = jnp.concatenate(
        [(lane_rows == lane[r : r + 1, :]).astype(F32).astype(BF16) for r in range(group_rows)], axis=1
    )
    in_block = [block_rows == block[r : r + 1, :] for r in range(group_rows)]
    found = jnp.dot(table3, hot, preferred_element_type=F32)
    count = 4 * seg_blocks
    found = found[0:count] + found[count : 2 * count] + found[2 * count : 3 * count]
    for f in range(4):
        field = found[f * seg_blocks : (f + 1) * seg_blocks]
        for r in range(group_rows):
            picked = jnp.where(in_block[r], field[:, r * BLK : (r + 1) * BLK], 0.0)
            values[f, r : r + 1, :] = jnp.sum(picked, axis=0, keepdims=True)
    tilt_x, tilt_y = values[0], values[1]
    unit = 1.0 / jnp.sqrt(1.0 + tilt_x * tilt_x + tilt_y * tilt_y)
    normal = (tilt_x * unit, tilt_y * unit, unit)
    depth = normal[0] * nodes[0] + normal[1] * nodes[1] + normal[2] * nodes[2] - values[2]
    pressure = jnp.where(valid, values[3] * jnp.maximum(depth, 0.0), 0.0)
    loads = [pressure * n for n in normal]
    for c in range(3):
        back_out[c] = loads[c]
    spread = jnp.concatenate(
        [
            jnp.concatenate([jnp.where(in_block[r], loads[c][r : r + 1, :], 0.0) for r in range(group_rows)], axis=1)
            for c in range(3)
        ],
        axis=0,
    )
    high = spread.astype(BF16)
    low = (spread - high.astype(F32)).astype(BF16)
    summed = lax.dot_general(
        jnp.concatenate([high, low], axis=0), hot, (((1,), (1,)), ((), ())), preferred_element_type=F32
    )
    summed = summed[0 : 3 * seg_blocks] + summed[3 * seg_blocks :]
    for c in range(3):
        for b in range(seg_blocks):
            at = c * seg_blocks + b
            react_ref[c : c + 1, b * BLK : (b + 1) * BLK] = summed[at : at + 1, :]

    def load_copy(off):
        return pltpu.make_async_remote_copy(
            src_ref=back_out.at[:, node_blocks * off : node_blocks * (off + 1), :],
            dst_ref=back.at[:, node_blocks * (off - 1) : node_blocks * off, :],
            send_sem=p2_send.at[off - 1],
            recv_sem=p2_recv.at[off - 1],
            device_id=(d, (s + sub_count - off) % sub_count),
            device_id_type=MESH,
        )

    for off in range(1, sub_count):
        load_copy(off).start()

    @pl.loop(early, (planes - 1) // group)
    def _(g):
        advance_group(g)

    for i, (dx, dy) in enumerate(DIRS):

        @pl.when(exists(-dx, -dy))
        def _():
            for copy in halo_copies(i):
                copy.wait_recv()

    for k, y in ((1, 0), (2, rows - 1)):
        for edge in (0, planes + 1):
            xr[k, :, edge, :] = w[:, edge, y, :]
    mx[1, 0:1, :] = md[0, rows - 1 : rows, :]

    node_plane(planes, element_plane(planes, inside_yz * (d < dom_count - 1).astype(F32)))
    force = element_plane(0, inside_yz * (d > 0).astype(F32))
    for m in range(3):
        for t in range(row_blocks):
            internal = part_of(force[t], m, 1, 0) + pltpu.roll(part_of(force[t], m, 1, 1), 1, 1)
            at = slice(8 * t, 8 * t + 8)
            nv_ref[m, 0, at, :] = nv_ref[m, 0, at, :] - step * internal

    height = planes + 8
    global_x = d * planes - 1 + iota((height, nz), 0)
    inside_xz = (
        (global_x >= 0) & (global_x <= planes * dom_count - 2) & (iota((height, nz), 1) <= nz - 2)
    ).astype(F32)
    for k, y, present in ((0, 0, s > 0), (1, rows - 1, s < sub_count - 1)):
        blocks = element_blocks(
            lambda f, a, b: xr[2 * k + b, f, a : a + height, :], mx[k], inside_xz * present.astype(F32)
        )
        here = mapped(edge_ref.at[2 * k], blocks[:-1])
        after = mapped(edge_ref.at[2 * k + 1], blocks[1:])
        for t in range(planes // 8):
            force = here[t] + after[t]
            for m in range(3):
                at = m * 16
                internal = step * (force[at : at + 8, :] + pltpu.roll(force[at + 8 : at + 16, :], 1, 1))
                for j in range(8):
                    x = 8 * t + j
                    nv_ref[m, x, y : y + 1, :] = nv_ref[m, x, y : y + 1, :] - internal[j : j + 1, :]

    for off in range(1, sub_count):
        load_copy(off).wait_recv()
    top = iota((nz, BLK), 0) == nz - 1
    for c in range(3):
        total = back_out[c, 0:node_blocks, :]
        for off in range(1, sub_count):
            total = total + back[c, node_blocks * (off - 1) : node_blocks * off, :]
        total = step * total
        for k in range(node_blocks):
            column = jnp.transpose(jnp.where(top, total[k : k + 1, :], 0.0)).reshape(block_planes, rows, nz)
            at = slice(k * block_planes, (k + 1) * block_planes)
            nv_ref[c, at, :, :] = nv_ref[c, at, :, :] - column

    for off in range(1, sub_count):
        node_copy(off).wait_send()
        load_copy(off).wait_send()
    for i, (dx, dy) in enumerate(DIRS):

        @pl.when(exists(dx, dy))
        def _():
            for copy in halo_copies(i):
                copy.wait_send()


def store_kernel(nv_ref, react_ref, nv_out, react_out, sem):
    copies = [
        pltpu.make_async_copy(a, b, sem.at[i]) for i, (a, b) in enumerate(((nv_ref, nv_out), (react_ref, react_out)))
    ]
    for copy in copies:
        copy.start()
    for copy in copies:
        copy.wait()


def local(
    dom_count, sub_count, displacement, velocity, modulus, element_stiffness, viscosity, step_size, seg_tilt,
    seg_offset, seg_stiffness, projection, contact_flag, candidates,
):
    _, planes, rows, nz = displacement.shape
    seg_local = seg_offset.shape[0]
    seg_blocks = seg_local // BLK
    node_blocks = projection.shape[0]
    group_rows = node_blocks * sub_count
    peers = sub_count - 1
    vmem = pl.BlockSpec(memory_space=pltpu.VMEM)
    hbm = pl.BlockSpec(memory_space=pl.ANY)
    dma = pltpu.SemaphoreType.DMA
    results = pl.pallas_call(
        functools.partial(kernel, dom_count, sub_count),
        out_shape=(
            pltpu.VMEM(velocity.shape, F32),
            pltpu.VMEM((3, seg_local), F32),
        ),
        in_specs=[hbm] * 12,
        out_specs=(vmem, vmem),
        scratch_shapes=[
            pltpu.SMEM((1,), F32),
            pltpu.SMEM((1,), F32),
            pltpu.VMEM(candidates.shape, jnp.int32),
            pltpu.VMEM(element_stiffness.shape, BF16),
            pltpu.VMEM(seg_tilt.shape, F32),
            pltpu.VMEM(projection.shape, jnp.int32),
            pltpu.VMEM(contact_flag.shape, jnp.int32),
            pltpu.VMEM((6, planes + 2, rows + 8, nz), F32),
            pltpu.VMEM((planes + 1, rows, nz), F32),
            pltpu.VMEM((4, 6, planes + 16, nz), F32),
            pltpu.VMEM((2, planes + 8, nz), F32),
            pltpu.VMEM((4, node_blocks, BLK), F32),
            pltpu.VMEM((4, group_rows, BLK), F32),
            pltpu.VMEM((3, group_rows, BLK), F32),
            pltpu.VMEM((3, node_blocks * peers, BLK), F32),
            pltpu.VMEM((4 * seg_blocks, BLK), F32),
            pltpu.VMEM((4, group_rows, BLK), F32),
            pltpu.VMEM((96, 192), BF16),
            pltpu.VMEM((96, 192), BF16),
            pltpu.VMEM((4, 48, 192), BF16),
            pltpu.VMEM((6, rows // 8, 8, nz), F32),
            dma((17,)),
            dma((8, 2)),
            dma((8, 2)),
            dma((peers,)),
            dma((peers,)),
            dma((peers,)),
            dma((peers,)),
        ],
        compiler_params=pltpu.CompilerParams(collective_id=0, has_side_effects=True),
    )(
        viscosity.reshape(1),
        step_size.reshape(1),
        candidates,
        element_stiffness,
        seg_tilt,
        seg_offset.reshape(seg_blocks, BLK),
        seg_stiffness.reshape(seg_blocks, BLK),
        projection,
        contact_flag,
        displacement,
        velocity,
        modulus,
    )
    return pl.pallas_call(
        store_kernel,
        out_shape=tuple(jax.ShapeDtypeStruct(x.shape, F32) for x in results),
        in_specs=[vmem, vmem],
        out_specs=(hbm, hbm),
        scratch_shapes=[dma((2,))],
    )(*(pltpu.with_memory_space_constraint(x, pltpu.VMEM) for x in results))


def solution(mesh):
    return jax.shard_map(
        functools.partial(local, mesh.shape["dom"], mesh.shape["sub"]),
        mesh=mesh,
        in_specs=(
            P(None, "dom", "sub", None),
            P(None, "dom", "sub", None),
            P("dom", "sub", None),
            P(),
            P(),
            P(),
            P(None, ("dom", "sub")),
            P(("dom", "sub")),
            P(("dom", "sub")),
            P(("dom", "sub"), None),
            P(("dom", "sub"), None),
            P(("dom", "sub"), None),
        ),
        out_specs=(P(None, "dom", "sub", None), P(None, ("dom", "sub"))),
        check_vma=False,
    )
```

profile of v0, /device:TPU:0, one launch (start us, length us, event | category | flops | bytes accessed | tf_op | source)
XLA Modules:
  0.0 13.4 jit_solution(4932869257280057777)
XLA Ops:
  1.9 10.7 %shard_map.131 = (f32[3,16,16,128]{3,2,1,0:T(8,128)S(1)}, f32[3,2048]{1,0:T(4,128)S(1)}) custom-call(f32[1]{0:T(128)} %bitcast.4.visc_hbm, f32[1]{0:T(128)} %bitcast.5.step_hbm, s32[2,8]{1,0:T(2,128)} %cand_hbm.1, bf16[24,24]{1,0:T(8,128)(2,1)} %stiff_hbm.1, f32[2,2048]{1,0:T(2,128)} %tilt_hbm.1, f32[16,128]{1,0:T(8,128)} %bitcast.6, f32[16,128]{1,0:T(8,128)} %bitcast.7, ...), custom_call_target="tpu_custom_call" | custom-call | tf_op jit(solution)/shard_map/pallas_call | solution.py:437
  12.6 0.8 %shard_map.132 = (f32[3,16,16,128]{3,2,1,0:T(8,128)}, f32[3,2048]{1,0:T(4,128)}) custom-call(f32[3,16,16,128]{3,2,1,0:T(8,128)S(1)} %get-tuple-element.4.nv_ref, f32[3,2048]{1,0:T(4,128)S(1)} %get-tuple-element.5.react_ref), custom_call_target="tpu_custom_call" | custom-call | tf_op jit(solution)/shard_map/pallas_call | solution.py:490
where the time goes:
time: 13.5 us; the launch traced here: 13.4 us
  Pallas kernels  11.4 us (84%)
  between operations  1.93 us (14%)
    pallas_call x1, Pallas kernels, local(): pl.pallas_call(functools.partial(kernel, dom_count, sub_count), out_shape...  10.7 us
    pallas_call x1, Pallas kernels, local(): pl.pallas_call(store_kernel, out_shape=tuple((jax.ShapeDtypeStruct(x.shap...  0.77 us

commit v1 on v0

--- a/solution.py
+++ b/solution.py
@@ -63,8 +63,8 @@
 def kernel(
     dom_count, sub_count, visc_hbm, step_hbm, cand_hbm, stiff_hbm, tilt_hbm, off_hbm, stf_hbm, proj_hbm, flag_hbm,
     disp, vel, mod, nv_ref, react_ref, visc_ref, step_ref, cand_ref, stiff_ref, tilt_ref, proj_ref, flag_ref,
-    w, md, xr, mx, msg, nodes, back_out, back, table, values, same_ref, carry_ref, edge_ref, prev,
-    local_sem, halo_send, halo_recv, p1_send, p1_recv, p2_send, p2_recv,
+    w, xr, msg, nodes, back_out, back, table, values, same_ref, carry_ref, edge_ref, prev,
+    local_sem, halo_send, halo_recv, peer_sem,
 ):
     d = lax.axis_index("dom")
     s = lax.axis_index("sub")
@@ -72,39 +72,52 @@
     inner = slice(1, 1 + planes)
     seg_blocks = off_hbm.shape[0]
     node_blocks = proj_ref.shape[0]
-    pairs = (
-        (disp, w.at[0:3, inner, 0:rows, :]),
-        (vel, w.at[3:6, inner, 0:rows, :]),
-        (mod, md.at[inner, :, :]),
-        (proj_hbm, proj_ref),
-        (flag_hbm, flag_ref),
-        (cand_hbm, cand_ref),
-        (stiff_hbm, stiff_ref),
-        (tilt_hbm, tilt_ref),
-        (off_hbm, table.at[2 * seg_blocks : 3 * seg_blocks, :]),
-        (stf_hbm, table.at[3 * seg_blocks : 4 * seg_blocks, :]),
-        (visc_hbm, visc_ref),
-        (step_hbm, step_ref),
-        (disp.at[:, :, 0, :], xr.at[1, 0:3, inner, :]),
-        (vel.at[:, :, 0, :], xr.at[1, 3:6, inner, :]),
-        (disp.at[:, :, rows - 1, :], xr.at[2, 0:3, inner, :]),
-        (vel.at[:, :, rows - 1, :], xr.at[2, 3:6, inner, :]),
-        (mod.at[:, rows - 1, :], mx.at[1, inner, :]),
+    own = w.at[:, inner, 0:rows, :]
+    stages = (
+        ("stiff", ((stiff_hbm, stiff_ref),), stiff_ref),
+        ("proj", ((proj_hbm, proj_ref),), proj_ref),
+        ("flag", ((flag_hbm, flag_ref),), flag_ref),
+        ("cand", ((cand_hbm, cand_ref),), cand_ref),
+        ("disp", ((disp, own.at[0:3]),), own.at[0:3]),
+        ("vel", ((vel, own.at[3:6]), (mod, own.at[6])), own.at[3:7]),
+        ("tilt", ((tilt_hbm, tilt_ref),), tilt_ref),
+        (
+            "table",
+            (
+                (off_hbm, table.at[2 * seg_blocks : 3 * seg_blocks, :]),
+                (stf_hbm, table.at[3 * seg_blocks : 4 * seg_blocks, :]),
+            ),
+            table.at[2 * seg_blocks : 4 * seg_blocks, :],
+        ),
+        ("visc", ((visc_hbm, visc_ref),), visc_ref),
+        ("step", ((step_hbm, step_ref),), step_ref),
+        (
+            "rows",
+            tuple(
+                copy
+                for k, y in ((1, 0), (2, rows - 1))
+                for copy in (
+                    (disp.at[:, :, y, :], xr.at[k, 0:3, inner, :]),
+                    (vel.at[:, :, y, :], xr.at[k, 3:6, inner, :]),
+                    (mod.at[:, y, :], xr.at[k, 6, inner, :]),
+                )
+            ),
+            xr.at[1:3, :, inner, :],
+        ),
     )
-    local_copies = [pltpu.make_async_copy(a, b, local_sem.at[i]) for i, (a, b) in enumerate(pairs)]
-    for copy in local_copies:
-        copy.start()
-
-    w[:, :, rows : rows + 8, :] = jnp.zeros((6, planes + 2, 8, nz), F32)
+    waits = {}
+    for i, (name, pairs, whole) in enumerate(stages):
+        for a, b in pairs:
+            pltpu.make_async_copy(a, b, local_sem.at[i]).start()
+        waits[name] = pltpu.make_async_copy(whole, whole, local_sem.at[i])
+
+    w[:, :, rows : rows + 8, :] = jnp.zeros((7, planes + 2, 8, nz), F32)
     for edge in (0, planes + 1):
-        w[:, edge, 0:rows, :] = jnp.zeros((6, rows, nz), F32)
-    md[0] = jnp.zeros((rows, nz), F32)
+        w[:, edge, 0:rows, :] = jnp.zeros((7, rows, nz), F32)
     for k in (0, 3):
         xr[k] = jnp.zeros(xr.shape[1:], F32)
     for k in (1, 2):
-        xr[k, :, planes + 1 :, :] = jnp.zeros((6, xr.shape[2] - planes - 1, nz), F32)
-    mx[0] = jnp.zeros(mx.shape[1:], F32)
-    mx[1, planes + 1 :, :] = jnp.zeros((mx.shape[1] - planes - 1, nz), F32)
+        xr[k, :, planes + 1 :, :] = jnp.zeros((7, xr.shape[2] - planes - 1, nz), F32)
 
     def exists(dx, dy):
         cond = (d + dx >= 0) & (d + dx < dom_count)
@@ -120,9 +133,17 @@
             def _():
                 pl.semaphore_signal(barrier, inc=1, device_id=(d + dx, s + dy), device_id_type=MESH)
 
-    for copy in local_copies:
-        copy.wait()
-
+    waits["stiff"].wait()
+    same, carry = stiffness_maps(stiff_ref[...])
+    same_ref[...] = same
+    carry_ref[...] = carry
+    for k in (0, 1):
+        same, following = edge_maps(stiff_ref[...], 1 - k)
+        edge_ref[2 * k] = same
+        edge_ref[2 * k + 1] = following
+
+    for name in ("proj", "flag", "cand", "disp"):
+        waits[name].wait()
     block_planes = BLK // rows
     group_start = d * (seg_blocks * BLK * sub_count)
     target = proj_ref[...] - group_start
@@ -137,70 +158,70 @@
             msg[c, k : k + 1, :] = jnp.transpose(part)[nz - 1 : nz, :]
     msg[3] = chosen
 
-    same, carry = stiffness_maps(stiff_ref[...])
-    same_ref[...] = same
-    carry_ref[...] = carry
-
+    columns = 1 + (s > 0).astype(jnp.int32) + (s < sub_count - 1).astype(jnp.int32)
+    sides = (d > 0).astype(jnp.int32) + (d < dom_count - 1).astype(jnp.int32)
+    pl.semaphore_wait(barrier, sub_count - 1 + columns * sides)
+
+    def node_copy(off):
+        return pltpu.make_async_remote_copy(
+            src_ref=msg,
+            dst_ref=nodes.at[:, node_blocks * off : node_blocks * (off + 1), :],
+            send_sem=peer_sem.at[0],
+            recv_sem=peer_sem.at[1],
+            device_id=(d, (s + off) % sub_count),
+            device_id_type=MESH,
+        )
+
+    for off in range(1, sub_count):
+        node_copy(off).start()
+    nodes_all = nodes.at[:, node_blocks : node_blocks * sub_count, :]
+    waits["nodes_sent"] = pltpu.make_async_copy(nodes_all, nodes_all, peer_sem.at[0])
+    waits["nodes"] = pltpu.make_async_copy(nodes_all, nodes_all, peer_sem.at[1])
+    waits["vel"].wait()
+
+    def halo_copy(dx, dy):
+        src_x = {1: planes, -1: 1, 0: inner}[dx]
+        dst_x = {1: 0, -1: planes + 1, 0: inner}[dx]
+        if dy == 0:
+            a, b = w.at[:, src_x, 0:rows, :], w.at[:, dst_x, 0:rows, :]
+        else:
+            a, b = w.at[:, src_x, rows - 1 if dy > 0 else 0, :], xr.at[0 if dy > 0 else 3, :, dst_x, :]
+        return pltpu.make_async_remote_copy(
+            src_ref=a,
+            dst_ref=b,
+            send_sem=halo_send.at[dx + 1],
+            recv_sem=halo_recv.at[dx + 1],
+            device_id=(d + dx, s + dy),
+            device_id_type=MESH,
+        )
+
+    for dx, dy in DIRS:
+
+        @pl.when(exists(dx, dy))
+        def _():
+            halo_copy(dx, dy).start()
+
+    def halo_wait(sem, sign):
+        both = (s > 0) & (s < sub_count - 1)
+        for dx in (-1, 0, 1):
+            for many, present in ((2, both), (1, jnp.logical_not(both))):
+                if dx == 0:
+                    part = w.at[:, 0:planes, 0:many, :]
+                else:
+                    part = w.at[:, 0 : rows + many, 0, :]
+
+                @pl.when(present & exists(sign * dx, 0))
+                def _():
+                    pltpu.make_async_copy(part, part, sem.at[dx + 1]).wait()
+
+    nodes[:, 0:node_blocks, :] = msg[...]
+    for name in ("tilt", "table", "visc", "step"):
+        waits[name].wait()
     for b in range(seg_blocks):
         lanes = slice(b * BLK, (b + 1) * BLK)
         for c in range(2):
             table[c * seg_blocks + b : c * seg_blocks + b + 1, :] = tilt_ref[c : c + 1, lanes]
     table3 = jnp.concatenate(split3(table[...]), axis=0)
-
-    columns = 1 + (s > 0).astype(jnp.int32) + (s < sub_count - 1).astype(jnp.int32)
-    sides = (d > 0).astype(jnp.int32) + (d < dom_count - 1).astype(jnp.int32)
-    pl.semaphore_wait(barrier, sub_count - 1 + columns * sides)
-
-    def halo_copies(i):
-        dx, dy = DIRS[i]
-        src_x = {1: planes, -1: 1, 0: inner}[dx]
-        dst_x = {1: 0, -1: planes + 1, 0: inner}[dx]
-        if dy == 0:
-            pairs = [(w.at[:, src_x, 0:rows, :], w.at[:, dst_x, 0:rows, :])]
-            if dx > 0:
-                pairs.append((md.at[src_x], md.at[dst_x]))
-        else:
-            src_y = rows - 1 if dy > 0 else 0
-            pairs = [(w.at[:, src_x, src_y, :], xr.at[0 if dy > 0 else 3, :, dst_x, :])]
-            if dx >= 0 and dy > 0:
-                pairs.append((md.at[src_x, src_y, :], mx.at[0, dst_x, :]))
-        return [
-            pltpu.make_async_remote_copy(
-                src_ref=a,
-                dst_ref=b,
-                send_sem=halo_send.at[i, j],
-                recv_sem=halo_recv.at[i, j],
-                device_id=(d + dx, s + dy),
-                device_id_type=MESH,
-            )
-            for j, (a, b) in enumerate(pairs)
-        ]
-
-    for i, (dx, dy) in enumerate(DIRS):
-
-        @pl.when(exists(dx, dy))
-        def _():
-            for copy in halo_copies(i):
-                copy.start()
-
-    def node_copy(off):
-        return pltpu.make_async_remote_copy(
-            src_ref=msg,
-            dst_ref=nodes.at[:, node_blocks * off : node_blocks * (off + 1), :],
-            send_sem=p1_send.at[off - 1],
-            recv_sem=p1_recv.at[off - 1],
-            device_id=(d, (s + off) % sub_count),
-            device_id_type=MESH,
-        )
-
-    for off in range(1, sub_count):
-        node_copy(off).start()
-    nodes[:, 0:node_blocks, :] = msg[...]
-
-    for k in (0, 1):
-        same, following = edge_maps(stiff_ref[...], 1 - k)
-        edge_ref[2 * k] = same
-        edge_ref[2 * k + 1] = following
 
     viscosity = visc_ref[0]
     step = step_ref[0]
@@ -244,7 +265,7 @@
     inside_yz = ((iota((rows, nz), 0) <= rows - 2) & (iota((rows, nz), 1) <= nz - 2)).astype(F32)
 
     def element_plane(e, mask):
-        blocks = element_blocks(lambda f, a, b: w[f, e + a, b : b + rows, :], md[e], mask)
+        blocks = element_blocks(lambda f, a, b: w[f, e + a, b : b + rows, :], w[6, e, 0:rows, :], mask)
         force = mapped(same_ref, blocks)
         carried = mapped(carry_ref, blocks[:-1]) if row_blocks > 1 else []
         return [force[0]] + [x + y for x, y in zip(force[1:], carried)]
@@ -281,8 +302,7 @@
     def _(g):
         advance_group(g)
 
-    for off in range(1, sub_count):
-        node_copy(off).wait_recv()
+    waits["nodes"].wait()
 
     group_rows = node_blocks * sub_count
     wanted = nodes[3].astype(jnp.int32) - s * (seg_blocks * BLK)
@@ -334,8 +354,8 @@
         return pltpu.make_async_remote_copy(
             src_ref=back_out.at[:, node_blocks * off : node_blocks * (off + 1), :],
             dst_ref=back.at[:, node_blocks * (off - 1) : node_blocks * off, :],
-            send_sem=p2_send.at[off - 1],
-            recv_sem=p2_recv.at[off - 1],
+            send_sem=peer_sem.at[2],
+            recv_sem=peer_sem.at[3],
             device_id=(d, (s + sub_count - off) % sub_count),
             device_id_type=MESH,
         )
@@ -347,17 +367,12 @@
     def _(g):
         advance_group(g)
 
-    for i, (dx, dy) in enumerate(DIRS):
-
-        @pl.when(exists(-dx, -dy))
-        def _():
-            for copy in halo_copies(i):
-                copy.wait_recv()
+    waits["rows"].wait()
+    halo_wait(halo_recv, -1)
 
     for k, y in ((1, 0), (2, rows - 1)):
         for edge in (0, planes + 1):
             xr[k, :, edge, :] = w[:, edge, y, :]
-    mx[1, 0:1, :] = md[0, rows - 1 : rows, :]
 
     node_plane(planes, element_plane(planes, inside_yz * (d < dom_count - 1).astype(F32)))
     force = element_plane(0, inside_yz * (d > 0).astype(F32))
@@ -374,7 +389,7 @@
     ).astype(F32)
     for k, y, present in ((0, 0, s > 0), (1, rows - 1, s < sub_count - 1)):
         blocks = element_blocks(
-            lambda f, a, b: xr[2 * k + b, f, a : a + height, :], mx[k], inside_xz * present.astype(F32)
+            lambda f, a, b: xr[2 * k + b, f, a : a + height, :], xr[2 * k, 6, 0:height, :], inside_xz * present.astype(F32)
         )
         here = mapped(edge_ref.at[2 * k], blocks[:-1])
         after = mapped(edge_ref.at[2 * k + 1], blocks[1:])
@@ -387,8 +402,7 @@
                     x = 8 * t + j
                     nv_ref[m, x, y : y + 1, :] = nv_ref[m, x, y : y + 1, :] - internal[j : j + 1, :]
 
-    for off in range(1, sub_count):
-        load_copy(off).wait_recv()
+    pltpu.make_async_copy(back, back, peer_sem.at[3]).wait()
     top = iota((nz, BLK), 0) == nz - 1
     for c in range(3):
         total = back_out[c, 0:node_blocks, :]
@@ -400,15 +414,9 @@
             at = slice(k * block_planes, (k + 1) * block_planes)
             nv_ref[c, at, :, :] = nv_ref[c, at, :, :] - column
 
-    for off in range(1, sub_count):
-        node_copy(off).wait_send()
-        load_copy(off).wait_send()
-    for i, (dx, dy) in enumerate(DIRS):
-
-        @pl.when(exists(dx, dy))
-        def _():
-            for copy in halo_copies(i):
-                copy.wait_send()
+    waits["nodes_sent"].wait()
+    pltpu.make_async_copy(back, back, peer_sem.at[2]).wait()
+    halo_wait(halo_send, 1)
 
 
 def store_kernel(nv_ref, react_ref, nv_out, react_out, sem):
@@ -450,10 +458,8 @@
             pltpu.VMEM(seg_tilt.shape, F32),
             pltpu.VMEM(projection.shape, jnp.int32),
             pltpu.VMEM(contact_flag.shape, jnp.int32),
-            pltpu.VMEM((6, planes + 2, rows + 8, nz), F32),
-            pltpu.VMEM((planes + 1, rows, nz), F32),
-            pltpu.VMEM((4, 6, planes + 16, nz), F32),
-            pltpu.VMEM((2, planes + 8, nz), F32),
+            pltpu.VMEM((7, planes + 2, rows + 8, nz), F32),
+            pltpu.VMEM((4, 7, planes + 16, nz), F32),
             pltpu.VMEM((4, node_blocks, BLK), F32),
             pltpu.VMEM((4, group_rows, BLK), F32),
             pltpu.VMEM((3, group_rows, BLK), F32),
@@ -464,13 +470,10 @@
             pltpu.VMEM((96, 192), BF16),
             pltpu.VMEM((4, 48, 192), BF16),
             pltpu.VMEM((6, rows // 8, 8, nz), F32),
-            dma((17,)),
-            dma((8, 2)),
-            dma((8, 2)),
-            dma((peers,)),
-            dma((peers,)),
-            dma((peers,)),
-            dma((peers,)),
+            dma((11,)),
+            dma((3,)),
+            dma((3,)),
+            dma((4,)),
         ],
         compiler_params=pltpu.CompilerParams(collective_id=0, has_side_effects=True),
     )(

time: 13.5 us -> 12.6 us (0.933)
  Pallas kernels: 11.4 us -> 10.4 us
    pallas_call x1, Pallas kernels: 10.7 us -> 9.64 us  [local(): pl.pallas_call(functools.partial(kernel, dom_count, sub_count), out_shape...]
where the time goes in v1:
time: 12.6 us; the launch traced here: 12.3 us
  Pallas kernels  10.4 us (83%)
  between operations  1.93 us (15%)
    pallas_call x1, Pallas kernels, local(): pl.pallas_call(functools.partial(kernel, dom_count, sub_count), out_shape...  9.64 us
    pallas_call x1, Pallas kernels, local(): pl.pallas_call(store_kernel, out_shape=tuple((jax.ShapeDtypeStruct(x.shap...  0.77 us

profile of v1, /device:TPU:0, one launch (start us, length us, event | category | flops | bytes accessed | tf_op | source)
XLA Modules:
  0.0 12.3 jit_solution(9151306810727407482)
XLA Ops:
  1.9 9.6 %shard_map.131 = (f32[3,16,16,128]{3,2,1,0:T(8,128)S(1)}, f32[3,2048]{1,0:T(4,128)S(1)}) custom-call(f32[1]{0:T(128)} %bitcast.4.visc_hbm, f32[1]{0:T(128)} %bitcast.5.step_hbm, s32[2,8]{1,0:T(2,128)} %cand_hbm.1, bf16[24,24]{1,0:T(8,128)(2,1)} %stiff_hbm.1, f32[2,2048]{1,0:T(2,128)} %tilt_hbm.1, f32[16,128]{1,0:T(8,128)} %bitcast.6, f32[16,128]{1,0:T(8,128)} %bitcast.7, ...), custom_call_target="tpu_custom_call" | custom-call | tf_op jit(solution)/shard_map/pallas_call | solution.py:445
  11.6 0.8 %shard_map.132 = (f32[3,16,16,128]{3,2,1,0:T(8,128)}, f32[3,2048]{1,0:T(4,128)}) custom-call(f32[3,16,16,128]{3,2,1,0:T(8,128)S(1)} %get-tuple-element.4.nv_ref, f32[3,2048]{1,0:T(4,128)S(1)} %get-tuple-element.5.react_ref), custom_call_target="tpu_custom_call" | custom-call | tf_op jit(solution)/shard_map/pallas_call | solution.py:493

commit v2 on v1

--- a/solution.py
+++ b/solution.py
@@ -10,7 +10,6 @@
 MESH = pl.DeviceIdType.MESH
 BLK = 128
 UNROLL = 3
-EARLY = 8
 F32 = jnp.float32
 BF16 = jnp.bfloat16
 DIRS = tuple((dx, dy) for dx in (-1, 0, 1) for dy in (-1, 0, 1) if (dx, dy) != (0, 0))
@@ -63,15 +62,31 @@
 def kernel(
     dom_count, sub_count, visc_hbm, step_hbm, cand_hbm, stiff_hbm, tilt_hbm, off_hbm, stf_hbm, proj_hbm, flag_hbm,
     disp, vel, mod, nv_ref, react_ref, visc_ref, step_ref, cand_ref, stiff_ref, tilt_ref, proj_ref, flag_ref,
-    w, xr, msg, nodes, back_out, back, table, values, same_ref, carry_ref, edge_ref, prev,
+    w, xr, xc, msg, nodes, tables, values, own_values, same_ref, carry_ref, edge_ref, prev,
     local_sem, halo_send, halo_recv, peer_sem,
 ):
     d = lax.axis_index("dom")
     s = lax.axis_index("sub")
     planes, rows, nz = disp.shape[1], disp.shape[2], disp.shape[3]
     inner = slice(1, 1 + planes)
+    table = tables.at[0]
     seg_blocks = off_hbm.shape[0]
     node_blocks = proj_ref.shape[0]
+    def exists(dx, dy):
+        cond = (d + dx >= 0) & (d + dx < dom_count)
+        return cond & (s + dy >= 0) & (s + dy < sub_count)
+
+    xc[...] = jnp.zeros(xc.shape, F32)
+    barrier = pltpu.get_barrier_semaphore()
+    for off in range(1, sub_count):
+        pl.semaphore_signal(barrier, inc=1, device_id=(d, (s + off) % sub_count), device_id_type=MESH)
+    for dx, dy in DIRS:
+        if dx != 0:
+
+            @pl.when(exists(dx, dy))
+            def _():
+                pl.semaphore_signal(barrier, inc=1, device_id=(d + dx, s + dy), device_id_type=MESH)
+
     own = w.at[:, inner, 0:rows, :]
     stages = (
         ("stiff", ((stiff_hbm, stiff_ref),), stiff_ref),
@@ -112,26 +127,20 @@
         waits[name] = pltpu.make_async_copy(whole, whole, local_sem.at[i])
 
     w[:, :, rows : rows + 8, :] = jnp.zeros((7, planes + 2, 8, nz), F32)
-    for edge in (0, planes + 1):
-        w[:, edge, 0:rows, :] = jnp.zeros((7, rows, nz), F32)
-    for k in (0, 3):
-        xr[k] = jnp.zeros(xr.shape[1:], F32)
-    for k in (1, 2):
+    for k in (0, 1, 2, 3):
+        xr[k, :, 0:1, :] = jnp.zeros((7, 1, nz), F32)
         xr[k, :, planes + 1 :, :] = jnp.zeros((7, xr.shape[2] - planes - 1, nz), F32)
-
-    def exists(dx, dy):
-        cond = (d + dx >= 0) & (d + dx < dom_count)
-        return cond & (s + dy >= 0) & (s + dy < sub_count)
-
-    barrier = pltpu.get_barrier_semaphore()
-    for off in range(1, sub_count):
-        pl.semaphore_signal(barrier, inc=1, device_id=(d, (s + off) % sub_count), device_id_type=MESH)
-    for dx, dy in DIRS:
-        if dx != 0:
-
-            @pl.when(exists(dx, dy))
-            def _():
-                pl.semaphore_signal(barrier, inc=1, device_id=(d + dx, s + dy), device_id_type=MESH)
+    for dx, edge in ((1, 0), (-1, planes + 1)):
+
+        @pl.when(jnp.logical_not(exists(-dx, 0)))
+        def _():
+            w[:, edge, 0:rows, :] = jnp.zeros((7, rows, nz), F32)
+
+    for dy, k in ((1, 0), (-1, 3)):
+
+        @pl.when(jnp.logical_not(exists(0, -dy)))
+        def _():
+            xr[k, :, 1 : planes + 1, :] = jnp.zeros((7, planes, nz), F32)
 
     waits["stiff"].wait()
     same, carry = stiffness_maps(stiff_ref[...])
@@ -158,9 +167,44 @@
             msg[c, k : k + 1, :] = jnp.transpose(part)[nz - 1 : nz, :]
     msg[3] = chosen
 
+    for name in ("tilt", "table", "visc", "step"):
+        waits[name].wait()
+    for b in range(seg_blocks):
+        lanes = slice(b * BLK, (b + 1) * BLK)
+        for c in range(2):
+            table[c * seg_blocks + b : c * seg_blocks + b + 1, :] = tilt_ref[c : c + 1, lanes]
     columns = 1 + (s > 0).astype(jnp.int32) + (s < sub_count - 1).astype(jnp.int32)
     sides = (d > 0).astype(jnp.int32) + (d < dom_count - 1).astype(jnp.int32)
     pl.semaphore_wait(barrier, sub_count - 1 + columns * sides)
+
+    waits["vel"].wait()
+
+    def halo_copy(dx, dy):
+        src_x = {1: planes, -1: 1, 0: inner}[dx]
+        dst_x = {1: 0, -1: planes + 1, 0: inner}[dx]
+        if dy == 0:
+            a, b = w.at[:, src_x, 0:rows, :], w.at[:, dst_x, 0:rows, :]
+        else:
+            k = 0 if dy > 0 else 3
+            a = w.at[:, src_x, rows - 1 if dy > 0 else 0, :]
+            b = xr.at[k, :, inner, :] if dx == 0 else xc.at[k, :, 0 if dx > 0 else 3, :]
+        return pltpu.make_async_remote_copy(
+            src_ref=a,
+            dst_ref=b,
+            send_sem=halo_send.at[dx + 1],
+            recv_sem=halo_recv.at[dx + 1],
+            device_id=(d + dx, s + dy),
+            device_id_type=MESH,
+        )
+
+    def send_halo(dirs):
+        for dx, dy in dirs:
+
+            @pl.when(exists(dx, dy))
+            def _():
+                halo_copy(dx, dy).start()
+
+    send_halo([(dx, dy) for dx, dy in DIRS if dy == 0])
 
     def node_copy(off):
         return pltpu.make_async_remote_copy(
@@ -174,36 +218,29 @@
 
     for off in range(1, sub_count):
         node_copy(off).start()
+    send_halo([(dx, dy) for dx, dy in DIRS if dy != 0])
+
+    def table_copy(off):
+        return pltpu.make_async_remote_copy(
+            src_ref=table,
+            dst_ref=tables.at[off],
+            send_sem=peer_sem.at[2],
+            recv_sem=peer_sem.at[3],
+            device_id=(d, (s + off) % sub_count),
+            device_id_type=MESH,
+        )
+
+    for off in range(1, sub_count):
+        table_copy(off).start()
+    received = tables.at[1:sub_count]
+    waits["tables_sent"] = pltpu.make_async_copy(received, received, peer_sem.at[2])
+    waits["tables"] = pltpu.make_async_copy(received, received, peer_sem.at[3])
     nodes_all = nodes.at[:, node_blocks : node_blocks * sub_count, :]
     waits["nodes_sent"] = pltpu.make_async_copy(nodes_all, nodes_all, peer_sem.at[0])
     waits["nodes"] = pltpu.make_async_copy(nodes_all, nodes_all, peer_sem.at[1])
-    waits["vel"].wait()
-
-    def halo_copy(dx, dy):
-        src_x = {1: planes, -1: 1, 0: inner}[dx]
-        dst_x = {1: 0, -1: planes + 1, 0: inner}[dx]
-        if dy == 0:
-            a, b = w.at[:, src_x, 0:rows, :], w.at[:, dst_x, 0:rows, :]
-        else:
-            a, b = w.at[:, src_x, rows - 1 if dy > 0 else 0, :], xr.at[0 if dy > 0 else 3, :, dst_x, :]
-        return pltpu.make_async_remote_copy(
-            src_ref=a,
-            dst_ref=b,
-            send_sem=halo_send.at[dx + 1],
-            recv_sem=halo_recv.at[dx + 1],
-            device_id=(d + dx, s + dy),
-            device_id_type=MESH,
-        )
-
-    for dx, dy in DIRS:
-
-        @pl.when(exists(dx, dy))
-        def _():
-            halo_copy(dx, dy).start()
-
-    def halo_wait(sem, sign):
+    def halo_wait(sem, sign, sides):
         both = (s > 0) & (s < sub_count - 1)
-        for dx in (-1, 0, 1):
+        for dx in sides:
             for many, present in ((2, both), (1, jnp.logical_not(both))):
                 if dx == 0:
                     part = w.at[:, 0:planes, 0:many, :]
@@ -215,14 +252,6 @@
                     pltpu.make_async_copy(part, part, sem.at[dx + 1]).wait()
 
     nodes[:, 0:node_blocks, :] = msg[...]
-    for name in ("tilt", "table", "visc", "step"):
-        waits[name].wait()
-    for b in range(seg_blocks):
-        lanes = slice(b * BLK, (b + 1) * BLK)
-        for c in range(2):
-            table[c * seg_blocks + b : c * seg_blocks + b + 1, :] = tilt_ref[c : c + 1, lanes]
-    table3 = jnp.concatenate(split3(table[...]), axis=0)
-
     viscosity = visc_ref[0]
     step = step_ref[0]
     row_blocks = rows // 8
@@ -292,46 +321,60 @@
 
     prev[...] = jnp.zeros(prev.shape, F32)
     group = UNROLL if (planes - 1) % UNROLL == 0 else 1
-    early = (planes - 1) // group * EARLY // 16
 
     def advance_group(g):
         for i in range(group):
             advance(1 + g * group + i)
 
-    @pl.loop(0, early)
+    @pl.loop(0, (planes - 1) // group)
     def _(g):
         advance_group(g)
 
+    for m in range(3):
+        for t in range(row_blocks):
+            internal = prev[m * 2, t] + pltpu.roll(prev[m * 2 + 1, t], 1, 1)
+            at = slice(8 * t, 8 * t + 8)
+            nv_ref[m, planes - 1, at, :] = w[3 + m, planes, at, :] - step * internal
+
     waits["nodes"].wait()
 
     group_rows = node_blocks * sub_count
+    lane_rows = iota((BLK, BLK), 0)
+
+    def one_hot(lane):
+        return jnp.concatenate(
+            [(lane_rows == lane[r : r + 1, :]).astype(F32).astype(BF16) for r in range(lane.shape[0])], axis=1
+        )
+
+    def contact(slots, store, hot, in_block, valid, place):
+        parts = jnp.concatenate(split3(tables[0:slots].reshape(slots * 4 * seg_blocks, BLK)), axis=0)
+        found = jnp.dot(parts, hot, preferred_element_type=F32)
+        count = slots * 4 * seg_blocks
+        found = found[0:count] + found[count : 2 * count] + found[2 * count : 3 * count]
+        for f in range(4):
+            for r in range(len(in_block)):
+                picked = None
+                for k in range(slots):
+                    at = (k * 4 + f) * seg_blocks
+                    field = found[at : at + seg_blocks, r * BLK : (r + 1) * BLK]
+                    term = jnp.where(in_block[r][k * seg_blocks : (k + 1) * seg_blocks], field, 0.0)
+                    picked = term if picked is None else picked + term
+                store[f, r : r + 1, :] = jnp.sum(picked, axis=0, keepdims=True)
+        tilt_x, tilt_y = store[0], store[1]
+        unit = 1.0 / jnp.sqrt(1.0 + tilt_x * tilt_x + tilt_y * tilt_y)
+        normal = (tilt_x * unit, tilt_y * unit, unit)
+        depth = normal[0] * place[0] + normal[1] * place[1] + normal[2] * place[2] - store[2]
+        pressure = jnp.where(valid, store[3] * jnp.maximum(depth, 0.0), 0.0)
+        return [pressure * n for n in normal]
+
     wanted = nodes[3].astype(jnp.int32) - s * (seg_blocks * BLK)
     valid = (nodes[3] >= 0.0) & (wanted >= 0) & (wanted < seg_blocks * BLK)
     wanted = jnp.where(valid, wanted, 0)
-    lane = wanted % BLK
     block = jnp.where(valid, wanted // BLK, -1)
-    lane_rows = iota((BLK, BLK), 0)
+    hot = one_hot(wanted % BLK)
     block_rows = iota((seg_blocks, BLK), 0)
-    hot = jnp.concatenate(
-        [(lane_rows == lane[r : r + 1, :]).astype(F32).astype(BF16) for r in range(group_rows)], axis=1
-    )
     in_block = [block_rows == block[r : r + 1, :] for r in range(group_rows)]
-    found = jnp.dot(table3, hot, preferred_element_type=F32)
-    count = 4 * seg_blocks
-    found = found[0:count] + found[count : 2 * count] + found[2 * count : 3 * count]
-    for f in range(4):
-        field = found[f * seg_blocks : (f + 1) * seg_blocks]
-        for r in range(group_rows):
-            picked = jnp.where(in_block[r], field[:, r * BLK : (r + 1) * BLK], 0.0)
-            values[f, r : r + 1, :] = jnp.sum(picked, axis=0, keepdims=True)
-    tilt_x, tilt_y = values[0], values[1]
-    unit = 1.0 / jnp.sqrt(1.0 + tilt_x * tilt_x + tilt_y * tilt_y)
-    normal = (tilt_x * unit, tilt_y * unit, unit)
-    depth = normal[0] * nodes[0] + normal[1] * nodes[1] + normal[2] * nodes[2] - values[2]
-    pressure = jnp.where(valid, values[3] * jnp.maximum(depth, 0.0), 0.0)
-    loads = [pressure * n for n in normal]
-    for c in range(3):
-        back_out[c] = loads[c]
+    loads = contact(1, values, hot, in_block, valid, nodes)
     spread = jnp.concatenate(
         [
             jnp.concatenate([jnp.where(in_block[r], loads[c][r : r + 1, :], 0.0) for r in range(group_rows)], axis=1)
@@ -350,51 +393,21 @@
             at = c * seg_blocks + b
             react_ref[c : c + 1, b * BLK : (b + 1) * BLK] = summed[at : at + 1, :]
 
-    def load_copy(off):
-        return pltpu.make_async_remote_copy(
-            src_ref=back_out.at[:, node_blocks * off : node_blocks * (off + 1), :],
-            dst_ref=back.at[:, node_blocks * (off - 1) : node_blocks * off, :],
-            send_sem=peer_sem.at[2],
-            recv_sem=peer_sem.at[3],
-            device_id=(d, (s + sub_count - off) % sub_count),
-            device_id_type=MESH,
+    waits["rows"].wait()
+    halo_wait(halo_recv, -1, (0,))
+    sides = ((0, 0, s > 0), (1, rows - 1, s < sub_count - 1))
+    along = iota((planes, nz), 0)
+    inside_xz = ((along >= 1) & (iota((planes, nz), 1) <= nz - 2)).astype(F32)
+    for k, y, present in sides:
+        blocks = element_blocks(
+            lambda f, a, b: xr[2 * k + b, f, a : a + planes, :],
+            xr[2 * k, 6, 0:planes, :],
+            inside_xz * present.astype(F32),
         )
-
-    for off in range(1, sub_count):
-        load_copy(off).start()
-
-    @pl.loop(early, (planes - 1) // group)
-    def _(g):
-        advance_group(g)
-
-    waits["rows"].wait()
-    halo_wait(halo_recv, -1)
-
-    for k, y in ((1, 0), (2, rows - 1)):
-        for edge in (0, planes + 1):
-            xr[k, :, edge, :] = w[:, edge, y, :]
-
-    node_plane(planes, element_plane(planes, inside_yz * (d < dom_count - 1).astype(F32)))
-    force = element_plane(0, inside_yz * (d > 0).astype(F32))
-    for m in range(3):
-        for t in range(row_blocks):
-            internal = part_of(force[t], m, 1, 0) + pltpu.roll(part_of(force[t], m, 1, 1), 1, 1)
-            at = slice(8 * t, 8 * t + 8)
-            nv_ref[m, 0, at, :] = nv_ref[m, 0, at, :] - step * internal
-
-    height = planes + 8
-    global_x = d * planes - 1 + iota((height, nz), 0)
-    inside_xz = (
-        (global_x >= 0) & (global_x <= planes * dom_count - 2) & (iota((height, nz), 1) <= nz - 2)
-    ).astype(F32)
-    for k, y, present in ((0, 0, s > 0), (1, rows - 1, s < sub_count - 1)):
-        blocks = element_blocks(
-            lambda f, a, b: xr[2 * k + b, f, a : a + height, :], xr[2 * k, 6, 0:height, :], inside_xz * present.astype(F32)
-        )
-        here = mapped(edge_ref.at[2 * k], blocks[:-1])
-        after = mapped(edge_ref.at[2 * k + 1], blocks[1:])
+        here = mapped(edge_ref.at[2 * k], blocks)
+        after = mapped(edge_ref.at[2 * k + 1], blocks[1:]) if planes > 8 else []
         for t in range(planes // 8):
-            force = here[t] + after[t]
+            force = here[t] + after[t] if t < len(after) else here[t]
             for m in range(3):
                 at = m * 16
                 internal = step * (force[at : at + 8, :] + pltpu.roll(force[at + 8 : at + 16, :], 1, 1))
@@ -402,21 +415,64 @@
                     x = 8 * t + j
                     nv_ref[m, x, y : y + 1, :] = nv_ref[m, x, y : y + 1, :] - internal[j : j + 1, :]
 
-    pltpu.make_async_copy(back, back, peer_sem.at[3]).wait()
+    own_valid = msg[3] >= 0.0
+    own_wanted = jnp.where(own_valid, msg[3].astype(jnp.int32), 0)
+    slot = (s + sub_count - own_wanted // (seg_blocks * BLK)) % sub_count
+    own_block = slot * seg_blocks + own_wanted % (seg_blocks * BLK) // BLK
+    own_block = jnp.where(own_valid, own_block, -1)
+    own_hot = one_hot(own_wanted % BLK)
+    own_rows = iota((sub_count * seg_blocks, BLK), 0)
+    own_in_block = [own_rows == own_block[r : r + 1, :] for r in range(node_blocks)]
+    waits["tables"].wait()
+    loads = contact(sub_count, own_values, own_hot, own_in_block, own_valid, msg)
     top = iota((nz, BLK), 0) == nz - 1
     for c in range(3):
-        total = back_out[c, 0:node_blocks, :]
-        for off in range(1, sub_count):
-            total = total + back[c, node_blocks * (off - 1) : node_blocks * off, :]
-        total = step * total
+        total = step * loads[c]
         for k in range(node_blocks):
             column = jnp.transpose(jnp.where(top, total[k : k + 1, :], 0.0)).reshape(block_planes, rows, nz)
             at = slice(k * block_planes, (k + 1) * block_planes)
             nv_ref[c, at, :, :] = nv_ref[c, at, :, :] - column
 
+    halo_wait(halo_recv, -1, (-1, 1))
+    for k, y in ((1, 0), (2, rows - 1)):
+        for edge, at in ((0, 0), (planes + 1, 3)):
+            xc[k, :, at, :] = w[:, edge, y, :]
+    for k in range(4):
+        for edge, at in ((1, 1), (planes, 2)):
+            xc[k, :, at, :] = xr[k, :, edge, :]
+
+    lower = (d > 0).astype(F32)
+    upper = (d < dom_count - 1).astype(F32)
+    ahead = element_plane(planes, inside_yz * upper)
+    behind = element_plane(0, inside_yz * lower)
+    pair = iota((8, nz), 0)
+    ends = jnp.where(pair == 0, lower, 0.0) + jnp.where(pair == 2, upper, 0.0)
+    ends = jnp.where(iota((8, nz), 1) <= nz - 2, ends, 0.0)
+    corners = [
+        mapped(
+            edge_ref.at[2 * k],
+            element_blocks(
+                lambda f, a, b: xc[2 * k + b, f, a : a + 8, :], xc[2 * k, 6, 0:8, :], ends * present.astype(F32)
+            ),
+        )[0]
+        for k, y, present in sides
+    ]
+    for force, a, x in ((ahead, 0, planes - 1), (behind, 1, 0)):
+        for m in range(3):
+            for t in range(row_blocks):
+                internal = part_of(force[t], m, a, 0) + pltpu.roll(part_of(force[t], m, a, 1), 1, 1)
+                at = slice(8 * t, 8 * t + 8)
+                nv_ref[m, x, at, :] = nv_ref[m, x, at, :] - step * internal
+    for (k, y, present), force in zip(sides, corners):
+        for m in range(3):
+            at = m * 16
+            internal = step * (force[at : at + 8, :] + pltpu.roll(force[at + 8 : at + 16, :], 1, 1))
+            for j, x in ((0, 0), (1, planes - 1)):
+                nv_ref[m, x, y : y + 1, :] = nv_ref[m, x, y : y + 1, :] - internal[j : j + 1, :]
+
     waits["nodes_sent"].wait()
-    pltpu.make_async_copy(back, back, peer_sem.at[2]).wait()
-    halo_wait(halo_send, 1)
+    waits["tables_sent"].wait()
+    halo_wait(halo_send, 1, (-1, 0, 1))
 
 
 def store_kernel(nv_ref, react_ref, nv_out, react_out, sem):
@@ -438,7 +494,6 @@
     seg_blocks = seg_local // BLK
     node_blocks = projection.shape[0]
     group_rows = node_blocks * sub_count
-    peers = sub_count - 1
     vmem = pl.BlockSpec(memory_space=pltpu.VMEM)
     hbm = pl.BlockSpec(memory_space=pl.ANY)
     dma = pltpu.SemaphoreType.DMA
@@ -460,12 +515,12 @@
             pltpu.VMEM(contact_flag.shape, jnp.int32),
             pltpu.VMEM((7, planes + 2, rows + 8, nz), F32),
             pltpu.VMEM((4, 7, planes + 16, nz), F32),
+            pltpu.VMEM((4, 7, 16, nz), F32),
             pltpu.VMEM((4, node_blocks, BLK), F32),
             pltpu.VMEM((4, group_rows, BLK), F32),
-            pltpu.VMEM((3, group_rows, BLK), F32),
-            pltpu.VMEM((3, node_blocks * peers, BLK), F32),
-            pltpu.VMEM((4 * seg_blocks, BLK), F32),
+            pltpu.VMEM((sub_count, 4 * seg_blocks, BLK), F32),
             pltpu.VMEM((4, group_rows, BLK), F32),
+            pltpu.VMEM((4, node_blocks, BLK), F32),
             pltpu.VMEM((96, 192), BF16),
             pltpu.VMEM((96, 192), BF16),
             pltpu.VMEM((4, 48, 192), BF16),

time: 12.6 us -> 11.4 us (0.905)
  Pallas kernels: 10.4 us -> 9.29 us
    pallas_call x1, Pallas kernels: 9.64 us -> 8.53 us  [local(): pl.pallas_call(functools.partial(kernel, dom_count, sub_count), out_shape...]
where the time goes in v2:
time: 11.4 us; the launch traced here: 11.2 us
  Pallas kernels  9.29 us (81%)
  between operations  1.93 us (17%)
    pallas_call x1, Pallas kernels, local(): pl.pallas_call(functools.partial(kernel, dom_count, sub_count), out_shape...  8.53 us
    pallas_call x1, Pallas kernels, local(): pl.pallas_call(store_kernel, out_shape=tuple((jax.ShapeDtypeStruct(x.shap...  0.77 us

profile of v2, /device:TPU:0, one launch (start us, length us, event | category | flops | bytes accessed | tf_op | source)
XLA Modules:
  0.0 11.2 jit_solution(16789766085162574445)
XLA Ops:
  1.9 8.5 %shard_map.131 = (f32[3,16,16,128]{3,2,1,0:T(8,128)S(1)}, f32[3,2048]{1,0:T(4,128)S(1)}) custom-call(f32[1]{0:T(128)} %bitcast.4.visc_hbm, f32[1]{0:T(128)} %bitcast.5.step_hbm, s32[2,8]{1,0:T(2,128)} %cand_hbm.1, bf16[24,24]{1,0:T(8,128)(2,1)} %stiff_hbm.1, f32[2,2048]{1,0:T(2,128)} %tilt_hbm.1, f32[16,128]{1,0:T(8,128)} %bitcast.6, f32[16,128]{1,0:T(8,128)} %bitcast.7, ...), custom_call_target="tpu_custom_call" | custom-call | tf_op jit(solution)/shard_map/pallas_call | solution.py:500
  10.5 0.8 %shard_map.132 = (f32[3,16,16,128]{3,2,1,0:T(8,128)}, f32[3,2048]{1,0:T(4,128)}) custom-call(f32[3,16,16,128]{3,2,1,0:T(8,128)S(1)} %get-tuple-element.4.nv_ref, f32[3,2048]{1,0:T(4,128)S(1)} %get-tuple-element.5.react_ref), custom_call_target="tpu_custom_call" | custom-call | tf_op jit(solution)/shard_map/pallas_call | solution.py:548

commit v3 on v2

--- a/solution.py
+++ b/solution.py
@@ -218,8 +218,6 @@
 
     for off in range(1, sub_count):
         node_copy(off).start()
-    send_halo([(dx, dy) for dx, dy in DIRS if dy != 0])
-
     def table_copy(off):
         return pltpu.make_async_remote_copy(
             src_ref=table,
@@ -232,6 +230,7 @@
 
     for off in range(1, sub_count):
         table_copy(off).start()
+    send_halo([(dx, dy) for dx, dy in DIRS if dy != 0])
     received = tables.at[1:sub_count]
     waits["tables_sent"] = pltpu.make_async_copy(received, received, peer_sem.at[2])
     waits["tables"] = pltpu.make_async_copy(received, received, peer_sem.at[3])
@@ -336,9 +335,6 @@
             at = slice(8 * t, 8 * t + 8)
             nv_ref[m, planes - 1, at, :] = w[3 + m, planes, at, :] - step * internal
 
-    waits["nodes"].wait()
-
-    group_rows = node_blocks * sub_count
     lane_rows = iota((BLK, BLK), 0)
 
     def one_hot(lane):
@@ -346,8 +342,20 @@
             [(lane_rows == lane[r : r + 1, :]).astype(F32).astype(BF16) for r in range(lane.shape[0])], axis=1
         )
 
-    def contact(slots, store, hot, in_block, valid, place):
-        parts = jnp.concatenate(split3(tables[0:slots].reshape(slots * 4 * seg_blocks, BLK)), axis=0)
+    own_valid = msg[3] >= 0.0
+    own_wanted = jnp.where(own_valid, msg[3].astype(jnp.int32), 0)
+    slot = (s + sub_count - own_wanted // (seg_blocks * BLK)) % sub_count
+    own_block = slot * seg_blocks + own_wanted % (seg_blocks * BLK) // BLK
+    own_block = jnp.where(own_valid, own_block, -1)
+    own_hot = one_hot(own_wanted % BLK)
+    own_rows = iota((sub_count * seg_blocks, BLK), 0)
+    own_in_block = [own_rows == own_block[r : r + 1, :] for r in range(node_blocks)]
+    own_parts = jnp.concatenate(split3(table[...]), axis=0)
+
+    waits["nodes"].wait()
+
+    group_rows = node_blocks * sub_count
+    def contact(slots, parts, store, hot, in_block, valid, place):
         found = jnp.dot(parts, hot, preferred_element_type=F32)
         count = slots * 4 * seg_blocks
         found = found[0:count] + found[count : 2 * count] + found[2 * count : 3 * count]
@@ -374,7 +382,7 @@
     hot = one_hot(wanted % BLK)
     block_rows = iota((seg_blocks, BLK), 0)
     in_block = [block_rows == block[r : r + 1, :] for r in range(group_rows)]
-    loads = contact(1, values, hot, in_block, valid, nodes)
+    loads = contact(1, own_parts, values, hot, in_block, valid, nodes)
     spread = jnp.concatenate(
         [
             jnp.concatenate([jnp.where(in_block[r], loads[c][r : r + 1, :], 0.0) for r in range(group_rows)], axis=1)
@@ -392,6 +400,17 @@
         for b in range(seg_blocks):
             at = c * seg_blocks + b
             react_ref[c : c + 1, b * BLK : (b + 1) * BLK] = summed[at : at + 1, :]
+
+    waits["tables"].wait()
+    parts = jnp.concatenate(split3(tables[...].reshape(sub_count * 4 * seg_blocks, BLK)), axis=0)
+    loads = contact(sub_count, parts, own_values, own_hot, own_in_block, own_valid, msg)
+    top = iota((nz, BLK), 0) == nz - 1
+    for c in range(3):
+        total = step * loads[c]
+        for k in range(node_blocks):
+            column = jnp.transpose(jnp.where(top, total[k : k + 1, :], 0.0)).reshape(block_planes, rows, nz)
+            at = slice(k * block_planes, (k + 1) * block_planes)
+            nv_ref[c, at, :, :] = nv_ref[c, at, :, :] - column
 
     waits["rows"].wait()
     halo_wait(halo_recv, -1, (0,))
@@ -414,24 +433,6 @@
                 for j in range(8):
                     x = 8 * t + j
                     nv_ref[m, x, y : y + 1, :] = nv_ref[m, x, y : y + 1, :] - internal[j : j + 1, :]
-
-    own_valid = msg[3] >= 0.0
-    own_wanted = jnp.where(own_valid, msg[3].astype(jnp.int32), 0)
-    slot = (s + sub_count - own_wanted // (seg_blocks * BLK)) % sub_count
-    own_block = slot * seg_blocks + own_wanted % (seg_blocks * BLK) // BLK
-    own_block = jnp.where(own_valid, own_block, -1)
-    own_hot = one_hot(own_wanted % BLK)
-    own_rows = iota((sub_count * seg_blocks, BLK), 0)
-    own_in_block = [own_rows == own_block[r : r + 1, :] for r in range(node_blocks)]
-    waits["tables"].wait()
-    loads = contact(sub_count, own_values, own_hot, own_in_block, own_valid, msg)
-    top = iota((nz, BLK), 0) == nz - 1
-    for c in range(3):
-        total = step * loads[c]
-        for k in range(node_blocks):
-            column = jnp.transpose(jnp.where(top, total[k : k + 1, :], 0.0)).reshape(block_planes, rows, nz)
-            at = slice(k * block_planes, (k + 1) * block_planes)
-            nv_ref[c, at, :, :] = nv_ref[c, at, :, :] - column
 
     halo_wait(halo_recv, -1, (-1, 1))
     for k, y in ((1, 0), (2, rows - 1)):

time: 11.4 us -> 11.2 us (0.982)
  Pallas kernels: 9.29 us -> 9.06 us
    pallas_call x1, Pallas kernels: 8.53 us -> 8.3 us  [local(): pl.pallas_call(functools.partial(kernel, dom_count, sub_count), out_shape...]
where the time goes in v3:
time: 11.2 us; the launch traced here: 11 us
  Pallas kernels  9.06 us (81%)
  between operations  1.93 us (17%)
    pallas_call x1, Pallas kernels, local(): pl.pallas_call(functools.partial(kernel, dom_count, sub_count), out_shape...  8.3 us
    pallas_call x1, Pallas kernels, local(): pl.pallas_call(store_kernel, out_shape=tuple((jax.ShapeDtypeStruct(x.shap...  0.77 us

profile of v3, /device:TPU:0, one launch (start us, length us, event | category | flops | bytes accessed | tf_op | source)
XLA Modules:
  0.0 11.0 jit_solution(13450555498808403005)
XLA Ops:
  1.9 8.3 %shard_map.131 = (f32[3,16,16,128]{3,2,1,0:T(8,128)S(1)}, f32[3,2048]{1,0:T(4,128)S(1)}) custom-call(f32[1]{0:T(128)} %bitcast.4.visc_hbm, f32[1]{0:T(128)} %bitcast.5.step_hbm, s32[2,8]{1,0:T(2,128)} %cand_hbm.1, bf16[24,24]{1,0:T(8,128)(2,1)} %stiff_hbm.1, f32[2,2048]{1,0:T(2,128)} %tilt_hbm.1, f32[16,128]{1,0:T(8,128)} %bitcast.6, f32[16,128]{1,0:T(8,128)} %bitcast.7, ...), custom_call_target="tpu_custom_call" | custom-call | tf_op jit(solution)/shard_map/pallas_call | solution.py:501
  10.2 0.8 %shard_map.132 = (f32[3,16,16,128]{3,2,1,0:T(8,128)}, f32[3,2048]{1,0:T(4,128)}) custom-call(f32[3,16,16,128]{3,2,1,0:T(8,128)S(1)} %get-tuple-element.4.nv_ref, f32[3,2048]{1,0:T(4,128)S(1)} %get-tuple-element.5.react_ref), custom_call_target="tpu_custom_call" | custom-call | tf_op jit(solution)/shard_map/pallas_call | solution.py:549

commit v4 on v3

--- a/solution.py
+++ b/solution.py
@@ -127,6 +127,7 @@
         waits[name] = pltpu.make_async_copy(whole, whole, local_sem.at[i])
 
     w[:, :, rows : rows + 8, :] = jnp.zeros((7, planes + 2, 8, nz), F32)
+    w[6, planes + 1, 0:rows, :] = jnp.zeros((rows, nz), F32)
     for k in (0, 1, 2, 3):
         xr[k, :, 0:1, :] = jnp.zeros((7, 1, nz), F32)
         xr[k, :, planes + 1 :, :] = jnp.zeros((7, xr.shape[2] - planes - 1, nz), F32)
@@ -134,7 +135,9 @@
 
         @pl.when(jnp.logical_not(exists(-dx, 0)))
         def _():
-            w[:, edge, 0:rows, :] = jnp.zeros((7, rows, nz), F32)
+            w[0:6, edge, 0:rows, :] = jnp.zeros((6, rows, nz), F32)
+            if dx > 0:
+                w[6, edge, 0:rows, :] = jnp.zeros((rows, nz), F32)
 
     for dy, k in ((1, 0), (-1, 3)):
 
@@ -182,12 +185,13 @@
     def halo_copy(dx, dy):
         src_x = {1: planes, -1: 1, 0: inner}[dx]
         dst_x = {1: 0, -1: planes + 1, 0: inner}[dx]
+        fields = slice(0, 6) if dx < 0 else slice(0, 7)
         if dy == 0:
-            a, b = w.at[:, src_x, 0:rows, :], w.at[:, dst_x, 0:rows, :]
+            a, b = w.at[fields, src_x, 0:rows, :], w.at[fields, dst_x, 0:rows, :]
         else:
             k = 0 if dy > 0 else 3
-            a = w.at[:, src_x, rows - 1 if dy > 0 else 0, :]
-            b = xr.at[k, :, inner, :] if dx == 0 else xc.at[k, :, 0 if dx > 0 else 3, :]
+            a = w.at[fields, src_x, rows - 1 if dy > 0 else 0, :]
+            b = xr.at[k, :, inner, :] if dx == 0 else xc.at[k, fields, 0 if dx > 0 else 3, :]
         return pltpu.make_async_remote_copy(
             src_ref=a,
             dst_ref=b,
@@ -244,7 +248,7 @@
                 if dx == 0:
                     part = w.at[:, 0:planes, 0:many, :]
                 else:
-                    part = w.at[:, 0 : rows + many, 0, :]
+                    part = w.at[0 : 6 if dx < 0 else 7, 0 : rows + many, 0, :]
 
                 @pl.when(present & exists(sign * dx, 0))
                 def _():
@@ -402,6 +406,8 @@
             react_ref[c : c + 1, b * BLK : (b + 1) * BLK] = summed[at : at + 1, :]
 
     waits["tables"].wait()
+    waits["rows"].wait()
+    halo_wait(halo_recv, -1, (0,))
     parts = jnp.concatenate(split3(tables[...].reshape(sub_count * 4 * seg_blocks, BLK)), axis=0)
     loads = contact(sub_count, parts, own_values, own_hot, own_in_block, own_valid, msg)
     top = iota((nz, BLK), 0) == nz - 1
@@ -412,8 +418,6 @@
             at = slice(k * block_planes, (k + 1) * block_planes)
             nv_ref[c, at, :, :] = nv_ref[c, at, :, :] - column
 
-    waits["rows"].wait()
-    halo_wait(halo_recv, -1, (0,))
     sides = ((0, 0, s > 0), (1, rows - 1, s < sub_count - 1))
     along = iota((planes, nz), 0)
     inside_xz = ((along >= 1) & (iota((planes, nz), 1) <= nz - 2)).astype(F32)

time: 11.2 us -> 11.2 us (level)
  the two profiles are of different devices: /device:TPU:0 before, /device:TPU:1 now
where the time goes in v4:
time: 11.2 us; the launch traced here: 11 us
  Pallas kernels  9.04 us (81%)
  between operations  1.93 us (17%)
    pallas_call x1, Pallas kernels, local(): pl.pallas_call(functools.partial(kernel, dom_count, sub_count), out_shape...  8.27 us
    pallas_call x1, Pallas kernels, local(): pl.pallas_call(store_kernel, out_shape=tuple((jax.ShapeDtypeStruct(x.shap...  0.77 us

profile of v4, /device:TPU:1, one launch (start us, length us, event | category | flops | bytes accessed | tf_op | source)
XLA Modules:
  0.0 11.0 jit_solution(17084127571476880483)
XLA Ops:
  1.9 8.3 %shard_map.131 = (f32[3,16,16,128]{3,2,1,0:T(8,128)S(1)}, f32[3,2048]{1,0:T(4,128)S(1)}) custom-call(f32[1]{0:T(128)} %bitcast.4.visc_hbm, f32[1]{0:T(128)} %bitcast.5.step_hbm, s32[2,8]{1,0:T(2,128)} %cand_hbm.1, bf16[24,24]{1,0:T(8,128)(2,1)} %stiff_hbm.1, f32[2,2048]{1,0:T(2,128)} %tilt_hbm.1, f32[16,128]{1,0:T(8,128)} %bitcast.6, f32[16,128]{1,0:T(8,128)} %bitcast.7, ...), custom_call_target="tpu_custom_call" | custom-call | tf_op jit(solution)/shard_map/pallas_call | solution.py:505
  10.2 0.8 %shard_map.132 = (f32[3,16,16,128]{3,2,1,0:T(8,128)}, f32[3,2048]{1,0:T(4,128)}) custom-call(f32[3,16,16,128]{3,2,1,0:T(8,128)S(1)} %get-tuple-element.4.nv_ref, f32[3,2048]{1,0:T(4,128)S(1)} %get-tuple-element.5.react_ref), custom_call_target="tpu_custom_call" | custom-call | tf_op jit(solution)/shard_map/pallas_call | solution.py:553
